TPU v7x, 32 devices: a whole 2x2x4 slice. The times are simulated.
32 devices in a mesh: shard: 8 (over y, x, core), replica: 4 (over z).
Axes of the slice: x: 2, y: 2, z: 4, core: 2. Of those that a mesh axis runs over, the one named last changes fastest.
Arguments:
- hidden: bfloat16 [8192, 768], P(('replica', 'shard')), may hold values from -6 to 6
- segment_ids: int32 [8192], P(('replica', 'shard')), may hold values from 0 to 63, as said below
- w_qkv: bfloat16 [768, 2304], P('shard'), may hold values from -0.21875 to 0.21875
- b_qv: bfloat16 [2, 768], P(None, 'shard'), may hold values from -3 to 3
- w_out: bfloat16 [768, 768], P('shard'), may hold values from -3 to 3
- b_out: bfloat16 [768], P('shard'), may hold values from -3 to 3
- gain1: bfloat16 [768], P('shard'), may hold values from 0.5 to 1.5
- shift1: bfloat16 [768], P('shard'), may hold values from -3 to 3
- w_in: bfloat16 [768, 3072], P('shard'), may hold values from -0.21875 to 0.21875
- b_in: bfloat16 [3072], P('shard'), may hold values from -3 to 3
- w_back: bfloat16 [3072, 768], P('shard'), may hold values from -0.21875 to 0.21875
- b_back: bfloat16 [768], P('shard'), may hold values from -3 to 3
- gain2: bfloat16 [768], P('shard'), may hold values from 0.5 to 1.5
- shift2: bfloat16 [768], P('shard'), may hold values from -3 to 3
- cotangent: float32 [8192, 768], P(('replica', 'shard')), may hold values from -6 to 6
Outputs:
- output: bfloat16 [8192, 768], P(('replica', 'shard'))
- d_hidden: float32 [8192, 768], P(('replica', 'shard'))
- grad_w_qkv: float32 [768, 2304], P('shard')
- grad_b_qv: float32 [2, 768], P(None, 'shard')
- grad_w_out: float32 [768, 768], P('shard')
- grad_b_out: float32 [768], P('shard')
- grad_gain1: float32 [768], P('shard')
- grad_shift1: float32 [768], P('shard')
- grad_w_in: float32 [768, 3072], P('shard')
- grad_b_in: float32 [3072], P('shard')
- grad_w_back: float32 [3072, 768], P('shard')
- grad_b_back: float32 [768], P('shard')
- grad_gain2: float32 [768], P('shard')
- grad_shift2: float32 [768], P('shard')
Inputs may be any that keep to these rules, and one draw needn't show every extreme that they name: `segment_ids`: ids never fall along the tokens. Sequence s (tokens s * 2048 to (s + 1) * 2048 - 1) holds exactly 16 documents with ids s * 16 to s * 16 + 15, one of them 1280 tokens long.
All inputs are finite; a program needn't handle non-finite values.
Results may differ from a plain program's by a relative error of at most 0.023.
Values may be sent and summed in bfloat16 or wider, within the bound.
A program may use at most 192 MiB of HBM per device.

v0:
```python
import math
import jax
import jax.numpy as jnp
from jax import lax
from jax.sharding import PartitionSpec as P

HEADS = 12
scale_factor = 0.125
norm_epsilon = 1e-05
masked_value = -1e30


def normalize(resid, gain, shift):
    mean_value = jnp.mean(resid, axis=-1, keepdims=True)
    centered = resid - mean_value
    variance = jnp.mean(centered * centered, axis=-1, keepdims=True)
    return centered * lax.rsqrt(variance + norm_epsilon) * gain + shift


def gelu_exact(values):
    return jax.nn.gelu(values, approximate=False)


def keep_state(state):
    return state


def block_size(count):
    return math.gcd(count, 512)


def masked_scores(query_heads, key_heads, query_segs, key_segs):
    scores = (
        jnp.einsum("qhd,khd->hqk", query_heads, key_heads, preferred_element_type=jnp.float32)
        * scale_factor
    )
    allowed = query_segs[:, None] == key_segs[None, :]
    return (scores, allowed[None])


def grad_block(
    query_heads, dctx_heads, log_total, delta, query_segs, key_heads, value_heads, key_segs
):
    scores, allowed = masked_scores(query_heads, key_heads, query_segs, key_segs)
    probs = jnp.where(allowed, jnp.exp(scores - log_total[:, :, None]), 0.0)
    d_prob = jnp.einsum("qhd,khd->hqk", dctx_heads, value_heads, preferred_element_type=jnp.float32)
    d_scores = (probs * (d_prob - delta[:, :, None])).astype(jnp.bfloat16)
    return (probs.astype(jnp.bfloat16), d_scores)


def body(
    hidden,
    segment_ids,
    w_qkv,
    b_qv,
    w_out,
    b_out,
    gain1,
    shift1,
    w_in,
    b_in,
    w_back,
    b_back,
    gain2,
    shift2,
    cotangent,
):
    tok_rows, width = hidden.shape
    heads = HEADS
    head_dim = width // heads
    seg_low = segment_ids[0]
    seg_high = segment_ids[-1]
    wq_full, wo_full, bqv_full, bo_full, g1_full, s1_full = (
        lax.all_gather(w_qkv, "shard", axis=0, tiled=True),
        lax.all_gather(w_out, "shard", axis=0, tiled=True),
        lax.all_gather(b_qv, "shard", axis=1, tiled=True),
        lax.all_gather(b_out, "shard", axis=0, tiled=True),
        lax.all_gather(gain1, "shard", axis=0, tiled=True),
        lax.all_gather(shift1, "shard", axis=0, tiled=True),
    )
    qkv = jnp.dot(hidden, wq_full, preferred_element_type=jnp.float32)
    bqv_wide = bqv_full.astype(jnp.float32)
    query = (qkv[:, :width] + bqv_wide[0]).astype(jnp.bfloat16)
    keys = qkv[:, width : 2 * width].astype(jnp.bfloat16)
    values = (qkv[:, 2 * width :] + bqv_wide[1]).astype(jnp.bfloat16)
    query_heads = query.reshape(tok_rows, heads, head_dim)
    key_local = keys.reshape(tok_rows, heads, head_dim)
    value_local = values.reshape(tok_rows, heads, head_dim)
    start_state = (
        jnp.full((heads, tok_rows), masked_value, jnp.float32),
        jnp.zeros((heads, tok_rows), jnp.float32),
        jnp.zeros((tok_rows, heads, head_dim), jnp.float32),
    )
    key_piece = lax.all_gather(keys, "shard", axis=0, tiled=True)
    value_piece = lax.all_gather(values, "shard", axis=0, tiled=True)
    seg_piece = lax.all_gather(segment_ids, "shard", axis=0, tiled=True)
    count = key_piece.shape[0]
    block = block_size(count)

    def forward_step(index, state):
        offset = index * block
        key_heads = lax.dynamic_slice_in_dim(key_piece, offset, block, 0).reshape(
            block, heads, head_dim
        )
        value_heads = lax.dynamic_slice_in_dim(value_piece, offset, block, 0).reshape(
            block, heads, head_dim
        )
        key_segs = lax.dynamic_slice_in_dim(seg_piece, offset, block, 0)

        def forward_update(state):
            running_max, running_sum, accum = state
            scores, allowed = masked_scores(query_heads, key_heads, segment_ids, key_segs)
            new_max = jnp.maximum(
                running_max, jnp.max(jnp.where(allowed, scores, masked_value), axis=-1)
            )
            factor = jnp.exp(running_max - new_max)
            weights = jnp.where(allowed, jnp.exp(scores - new_max[:, :, None]), 0.0)
            running_sum = running_sum * factor + jnp.sum(weights, axis=-1)
            accum = accum * factor.T[:, :, None] + jnp.einsum(
                "hqk,khd->qhd",
                weights.astype(jnp.bfloat16),
                value_heads,
                preferred_element_type=jnp.float32,
            )
            return (new_max, running_sum, accum)

        touches = jnp.logical_and(key_segs[0] <= seg_high, key_segs[-1] >= seg_low)
        return lax.cond(touches, forward_update, keep_state, state)

    running_max, running_sum, accum = lax.fori_loop(0, count // block, forward_step, start_state)
    context32 = accum / running_sum.T[:, :, None]
    log_total = running_max + jnp.log(running_sum)
    context = context32.reshape(tok_rows, width).astype(jnp.bfloat16)
    resid1 = (
        hidden.astype(jnp.float32)
        + jnp.dot(context, wo_full, preferred_element_type=jnp.float32)
        + bo_full.astype(jnp.float32)
    )
    normed1, norm1_pull = jax.vjp(
        normalize, resid1, g1_full.astype(jnp.float32), s1_full.astype(jnp.float32)
    )
    wi_full, bi_full, wb_full, bb_full, g2_full, s2_full = (
        lax.all_gather(w_in, "shard", axis=0, tiled=True),
        lax.all_gather(b_in, "shard", axis=0, tiled=True),
        lax.all_gather(w_back, "shard", axis=0, tiled=True),
        lax.all_gather(b_back, "shard", axis=0, tiled=True),
        lax.all_gather(gain2, "shard", axis=0, tiled=True),
        lax.all_gather(shift2, "shard", axis=0, tiled=True),
    )
    normed1_low = normed1.astype(jnp.bfloat16)
    pre = jnp.dot(normed1_low, wi_full, preferred_element_type=jnp.float32) + bi_full.astype(
        jnp.float32
    )
    act, gelu_pull = jax.vjp(gelu_exact, pre)
    act_low = act.astype(jnp.bfloat16)
    resid2 = (
        normed1
        + jnp.dot(act_low, wb_full, preferred_element_type=jnp.float32)
        + bb_full.astype(jnp.float32)
    )
    out32, norm2_pull = jax.vjp(
        normalize, resid2, g2_full.astype(jnp.float32), s2_full.astype(jnp.float32)
    )
    output = out32.astype(jnp.bfloat16)
    d_resid2, grad_gain2, grad_shift2 = norm2_pull(cotangent)
    d_branch2 = d_resid2.astype(jnp.bfloat16)
    grad_b_back = jnp.sum(d_resid2, axis=0)
    grad_w_back = jnp.einsum("tf,td->fd", act_low, d_branch2, preferred_element_type=jnp.float32)
    d_act = jnp.einsum("td,fd->tf", d_branch2, wb_full, preferred_element_type=jnp.float32)
    (d_pre,) = gelu_pull(d_act)
    grad_b_in = jnp.sum(d_pre, axis=0)
    d_pre_low = d_pre.astype(jnp.bfloat16)
    grad_w_in = jnp.einsum("td,tf->df", normed1_low, d_pre_low, preferred_element_type=jnp.float32)
    d_normed1 = d_resid2 + jnp.einsum(
        "tf,df->td", d_pre_low, wi_full, preferred_element_type=jnp.float32
    )
    d_resid1, grad_gain1, grad_shift1 = norm1_pull(d_normed1)
    grad_b_out = jnp.sum(d_resid1, axis=0)
    d_branch1 = d_resid1.astype(jnp.bfloat16)
    grad_w_out = jnp.einsum("tc,td->cd", context, d_branch1, preferred_element_type=jnp.float32)
    d_context = jnp.einsum(
        "td,cd->tc", d_branch1, wo_full, preferred_element_type=jnp.float32
    ).astype(jnp.bfloat16)
    dctx_heads = d_context.reshape(tok_rows, heads, head_dim)
    delta = jnp.einsum("qhd,qhd->hq", dctx_heads.astype(jnp.float32), context32)
    zero_heads = jnp.zeros((tok_rows, heads, head_dim), jnp.float32)
    query_key_piece = lax.all_gather(keys, "shard", axis=0, tiled=True)
    query_value_piece = lax.all_gather(values, "shard", axis=0, tiled=True)
    query_seg_piece = lax.all_gather(segment_ids, "shard", axis=0, tiled=True)
    count = query_key_piece.shape[0]
    query_block = block_size(count)

    def query_step(index, summed):
        offset = index * query_block
        key_heads = lax.dynamic_slice_in_dim(query_key_piece, offset, query_block, 0).reshape(
            query_block, heads, head_dim
        )
        value_heads = lax.dynamic_slice_in_dim(query_value_piece, offset, query_block, 0).reshape(
            query_block, heads, head_dim
        )
        key_segs = lax.dynamic_slice_in_dim(query_seg_piece, offset, query_block, 0)

        def query_update(summed):
            probs, d_scores = grad_block(
                query_heads,
                dctx_heads,
                log_total,
                delta,
                segment_ids,
                key_heads,
                value_heads,
                key_segs,
            )
            return (
                summed
                + jnp.einsum(
                    "hqk,khd->qhd", d_scores, key_heads, preferred_element_type=jnp.float32
                )
                * scale_factor
            )

        touches = jnp.logical_and(key_segs[0] <= seg_high, key_segs[-1] >= seg_low)
        return lax.cond(touches, query_update, keep_state, summed)

    d_query = lax.fori_loop(0, count // query_block, query_step, zero_heads)
    all_log_total, all_delta = (
        lax.all_gather(log_total, "shard", axis=1, tiled=True),
        lax.all_gather(delta, "shard", axis=1, tiled=True),
    )
    query_piece = lax.all_gather(query, "shard", axis=0, tiled=True)
    dctx_piece = lax.all_gather(d_context, "shard", axis=0, tiled=True)
    key_seg_piece = lax.all_gather(segment_ids, "shard", axis=0, tiled=True)
    count = query_piece.shape[0]
    key_block = block_size(count)

    def key_step(index, state):
        offset = index * key_block
        piece_query = lax.dynamic_slice_in_dim(query_piece, offset, key_block, 0).reshape(
            key_block, heads, head_dim
        )
        piece_dctx = lax.dynamic_slice_in_dim(dctx_piece, offset, key_block, 0).reshape(
            key_block, heads, head_dim
        )
        piece_segs = lax.dynamic_slice_in_dim(key_seg_piece, offset, key_block, 0)
        piece_log = lax.dynamic_slice_in_dim(all_log_total, offset, key_block, 1)
        piece_delta = lax.dynamic_slice_in_dim(all_delta, offset, key_block, 1)

        def key_update(state):
            d_key, d_value = state
            probs, d_scores = grad_block(
                piece_query,
                piece_dctx,
                piece_log,
                piece_delta,
                piece_segs,
                key_local,
                value_local,
                segment_ids,
            )
            d_key = (
                d_key
                + jnp.einsum(
                    "hqk,qhd->khd", d_scores, piece_query, preferred_element_type=jnp.float32
                )
                * scale_factor
            )
            d_value = d_value + jnp.einsum(
                "hqk,qhd->khd", probs, piece_dctx, preferred_element_type=jnp.float32
            )
            return (d_key, d_value)

        touches = jnp.logical_and(piece_segs[0] <= seg_high, piece_segs[-1] >= seg_low)
        return lax.cond(touches, key_update, keep_state, state)

    d_key_heads, d_value_heads = lax.fori_loop(
        0, count // key_block, key_step, (zero_heads, zero_heads)
    )
    d_keys = d_key_heads.reshape(tok_rows, width)
    d_values = d_value_heads.reshape(tok_rows, width)
    d_query = d_query.reshape(tok_rows, width)
    grad_b_qv = jnp.stack([jnp.sum(d_query, axis=0), jnp.sum(d_values, axis=0)], axis=0)
    d_qkv = jnp.concatenate([d_query, d_keys, d_values], axis=1).astype(jnp.bfloat16)
    grad_w_qkv = jnp.einsum("td,te->de", hidden, d_qkv, preferred_element_type=jnp.float32)
    d_hidden = d_resid1 + jnp.einsum(
        "te,de->td", d_qkv, wq_full, preferred_element_type=jnp.float32
    )
    local_grads = (
        grad_w_qkv,
        grad_b_qv,
        grad_w_out,
        grad_b_out,
        grad_gain1,
        grad_shift1,
        grad_w_in,
        grad_b_in,
        grad_w_back,
        grad_b_back,
        grad_gain2,
        grad_shift2,
    )
    shard_grads = (
        lax.psum_scatter(
            local_grads[0].astype(jnp.bfloat16), "shard", scatter_dimension=0, tiled=True
        ).astype(jnp.float32),
        lax.psum_scatter(
            local_grads[1].astype(jnp.bfloat16), "shard", scatter_dimension=1, tiled=True
        ).astype(jnp.float32),
        lax.psum_scatter(
            local_grads[2].astype(jnp.bfloat16), "shard", scatter_dimension=0, tiled=True
        ).astype(jnp.float32),
        lax.psum_scatter(
            local_grads[3].astype(jnp.bfloat16), "shard", scatter_dimension=0, tiled=True
        ).astype(jnp.float32),
        lax.psum_scatter(
            local_grads[4].astype(jnp.bfloat16), "shard", scatter_dimension=0, tiled=True
        ).astype(jnp.float32),
        lax.psum_scatter(
            local_grads[5].astype(jnp.bfloat16), "shard", scatter_dimension=0, tiled=True
        ).astype(jnp.float32),
        lax.psum_scatter(
            local_grads[6].astype(jnp.bfloat16), "shard", scatter_dimension=0, tiled=True
        ).astype(jnp.float32),
        lax.psum_scatter(
            local_grads[7].astype(jnp.bfloat16), "shard", scatter_dimension=0, tiled=True
        ).astype(jnp.float32),
        lax.psum_scatter(
            local_grads[8].astype(jnp.bfloat16), "shard", scatter_dimension=0, tiled=True
        ).astype(jnp.float32),
        lax.psum_scatter(
            local_grads[9].astype(jnp.bfloat16), "shard", scatter_dimension=0, tiled=True
        ).astype(jnp.float32),
        lax.psum_scatter(
            local_grads[10].astype(jnp.bfloat16), "shard", scatter_dimension=0, tiled=True
        ).astype(jnp.float32),
        lax.psum_scatter(
            local_grads[11].astype(jnp.bfloat16), "shard", scatter_dimension=0, tiled=True
        ).astype(jnp.float32),
    )
    total_grads = (
        lax.psum(shard_grads[0].astype(jnp.bfloat16), "replica").astype(jnp.float32),
        lax.psum(shard_grads[1].astype(jnp.bfloat16), "replica").astype(jnp.float32),
        lax.psum(shard_grads[2].astype(jnp.bfloat16), "replica").astype(jnp.float32),
        lax.psum(shard_grads[3].astype(jnp.bfloat16), "replica").astype(jnp.float32),
        lax.psum(shard_grads[4].astype(jnp.bfloat16), "replica").astype(jnp.float32),
        lax.psum(shard_grads[5].astype(jnp.bfloat16), "replica").astype(jnp.float32),
        lax.psum(shard_grads[6].astype(jnp.bfloat16), "replica").astype(jnp.float32),
        lax.psum(shard_grads[7].astype(jnp.bfloat16), "replica").astype(jnp.float32),
        lax.psum(shard_grads[8].astype(jnp.bfloat16), "replica").astype(jnp.float32),
        lax.psum(shard_grads[9].astype(jnp.bfloat16), "replica").astype(jnp.float32),
        lax.psum(shard_grads[10].astype(jnp.bfloat16), "replica").astype(jnp.float32),
        lax.psum(shard_grads[11].astype(jnp.bfloat16), "replica").astype(jnp.float32),
    )
    return (output, d_hidden) + tuple(total_grads)


def solution(mesh):
    in_specs = (
        P(("replica", "shard"), None),
        P(("replica", "shard")),
        P("shard", None),
        P(None, "shard"),
        P("shard", None),
        P("shard"),
        P("shard"),
        P("shard"),
        P("shard", None),
        P("shard"),
        P("shard", None),
        P("shard"),
        P("shard"),
        P("shard"),
        P(("replica", "shard"), None),
    )
    out_specs = (
        P(("replica", "shard"), None),
        P(("replica", "shard"), None),
        P("shard", None),
        P(None, "shard"),
        P("shard", None),
        P("shard"),
        P("shard"),
        P("shard"),
        P("shard", None),
        P("shard"),
        P("shard", None),
        P("shard"),
        P("shard"),
        P("shard"),
    )
    return jax.shard_map(body, mesh=mesh, in_specs=in_specs, out_specs=out_specs, check_vma=False)
```

profile of v0, /device:TPU:0, one launch (start us, length us, event | category | flops | bytes accessed | tf_op | source)
XLA Modules:
  0.0 788.4 jit_solution(2066285224074038387)
XLA Ops:
  8.0 38.5 %all-gather.12.cloned.1.call-done = bf16[768,2304]{1,0:T(8,128)(2,1)} async-done(((bf16[96,2304]{1,0:T(8,128)(2,1)}), bf16[768,2304]{1,0:T(8,128)(2,1)}) %all-gather.12.cloned.1.call-update) | async-done | bytes 3538960 | tf_op jit(solution)/shard_map/all_gather | solution.py:74
  46.5 3.2 fusion.93
  50.7 8.7 %all-gather.1 = bf16[8,96,2]{1,2,0:T(2,128)(2,1)S(1)} all-gather(bf16[1,96,2]{1,2,0:T(2,128)(2,1)S(1)} %bitcast.172), channel_id=1, replica_groups=mesh['shard'=8,'replica'=4] {'shard'}, dimensions={0}, use_global_device_ids=true | all-gather | bytes 3456 | tf_op jit(solution)/shard_map/all_gather | solution.py:76
  64.7 24.2 %all-reduce.14 = (bf16[768]{0:T(1024)(128)(2,1)S(1)}, bf16[768]{0:T(1024)(128)(2,1)S(1)}, bf16[768]{0:T(1024)(128)(2,1)S(1)}, bf16[768]{0:T(1024)(128)(2,1)S(1)}, bf16[768]{0:T(1024)(128)(2,1)S(1)}) all-reduce(bf16[768]{0:T(1024)(128)(2,1)S(1)} %dynamic-update-slice, ...), channel_id=1, replica_groups=mesh['shard'=8,'replica'=4] {'shard'}, use_global_device_ids=true, to_apply=%add | all-reduce | flops 3840 | bytes 15360
  88.8 8.1 %all-gather.2 = bf16[8,1,384]{2,1,0:T(2,128)(2,1)S(1)} all-gather(bf16[1,1,384]{2,1,0:T(2,128)(2,1)S(1)} %reshape.302), channel_id=1, replica_groups=mesh['shard'=8,'replica'=4] {'shard'}, dimensions={0}, use_global_device_ids=true | all-gather | bytes 6912 | tf_op jit(solution)/shard_map/all_gather | solution.py:144
  97.0 8.8 %all-gather = s32[8,1,256]{2,1,0:T(1,128)} all-gather(s32[1,1,256]{2,1,0:T(1,128)S(1)} %bitcast.168), channel_id=1, replica_groups=mesh['shard'=8,'replica'=4] {'shard'}, dimensions={0}, use_global_device_ids=true | all-gather | bytes 9216 | tf_op jit(solution)/shard_map/all_gather | solution.py:96
  107.0 4.7 copy.72
  111.7 6.1 all-gather.16.cloned.1.call-done
  117.8 4.8 copy.73
  122.7 32.9 %while.48 = (s32[]{:T(128)}, f32[12,256]{1,0:T(8,128)S(1)}, f32[12,256]{1,0:T(8,128)S(1)}, f32[256,12,64]{0,2,1:T(8,128)S(1)}, s32[2048]{0:T(1024)}, /*index=5*/...) while((s32[]{:T(128)}, f32[12,256]{1,0:T(8,128)S(1)}, ...), condition=%wide.region_5.6_spmd, body=%wide.region_0.5_spmd.sunk | while | flops 420488192 | bytes 26287476 | solution.py:130
  126.7 5.7 conditional.6
  136.3 5.6 conditional.6
  145.9 5.6 conditional.6
  158.3 25.8 %all-gather.20.cloned.1.call-done = bf16[768,3072]{1,0:T(8,128)(2,1)} async-done(((bf16[96,3072]{1,0:T(8,128)(2,1)}), bf16[768,3072]{1,0:T(8,128)(2,1)}) %all-gather.20.cloned.1.call-update) | async-done | bytes 4718608 | tf_op jit(solution)/shard_map/all_gather | solution.py:143
  184.0 12.1 %multiply_convert_fusion.8 = (bf16[256,3072]{1,0:T(8,128)(2,1)}, f32[256,3072]{1,0:T(8,128)}, f32[256,3072]{1,0:T(8,128)}) fusion(f32[3072]{0:T(1024)S(1)} %bitcast.171, bf16[768,3072]{1,0:T(8,128)(2,1)} %all-gather.20.cloned.1.call-done, f32[256,768]{1,0:T(8,128)S(1)} %get-tuple-element.1246, f32[768]{0:T(1024)S(1)} %convert_element_type.209, ...), kind=kOutput, calls=%fused_computation.63 | convolution fusion | flops 1260847104 | bytes 13389824 | tf_op jit(solution)/shard_map/dot_general | solution.py:151
  196.1 28.4 %all-gather.22.cloned.1.call-done = bf16[3072,768]{1,0:T(8,128)(2,1)} async-done(((bf16[384,768]{1,0:T(8,128)(2,1)}), bf16[3072,768]{1,0:T(8,128)(2,1)}) %all-gather.22.cloned.1.call-update) | async-done | bytes 4718608 | tf_op jit(solution)/shard_map/all_gather | solution.py:145
  224.6 4.5 fusion.89
  231.5 2.8 fusion.90
  234.3 2.3 multiply_reduce_fusion.1
  242.4 16.2 %all-gather.24.cloned.1.call-done = bf16[2048,768]{1,0:T(8,128)(2,1)} async-done(((bf16[256,768]{1,0:T(8,128)(2,1)}), bf16[2048,768]{1,0:T(8,128)(2,1)}) %all-gather.24.cloned.1.call-update) | async-done | bytes 3145744 | tf_op jit(solution)/shard_map/all_gather | solution.py:230
  258.7 4.8 copy.79
  264.1 9.3 %all_gather.77 = f32[12,2048]{1,0:T(8,128)S(1)} all-gather(f32[12,256]{1,0:T(8,128)} %log_add_fusion), channel_id=1, replica_groups=mesh['shard'=8,'replica'=4] {'shard'}, dimensions={1}, use_global_device_ids=true | all-gather | bytes 110592 | tf_op jit(solution)/shard_map/all_gather | solution.py:227
  275.1 8.6 %all_gather.79 = f32[12,2048]{1,0:T(8,128)S(1)} all-gather(f32[12,256]{1,0:T(8,128)} %fusion.66), channel_id=1, replica_groups=mesh['shard'=8,'replica'=4] {'shard'}, dimensions={1}, use_global_device_ids=true | all-gather | bytes 110592 | tf_op jit(solution)/shard_map/all_gather | solution.py:228
  284.6 51.7 %while.49 = (s32[]{:T(128)}, f32[256,12,64]{0,2,1:T(8,128)}, s32[2048]{0:T(1024)}, s32[]{:T(128)}, s32[]{:T(128)}, /*index=5*/s32[256]{0:T(256)}, bf16[2048,768]...) while((s32[]{:T(128)}, f32[256,12,64]{0,2,1:T(8,128)}, ...), condition=%wide.region_17.18_spmd, body=%wide.region_14.17_spmd.sunk | while | flops 613941248 | bytes 20745584 | solution.py:225
  288.8 11.8 %conditional.7 = (f32[256,12,64]{0,2,1:T(8,128)}) conditional(s32[]{:T(128)} %convert_element_type.315, f32[256,12,64]{0,2,1:T(8,128)} %get-tuple-element.1570, (s32[256]{0:T(256)}, s32[512]{0:T(512)S(1)}, bf16[2048,768]{0,1:T(8,128)(2,1)}, s32[]{:T(128)}, bf16[256,12,64]{0,2,1:T(8,128)(2,1)S(1)}, /*index=5*/f32[12,256]{1,0:T(8,128)}, ...), branch_computations={%region_15.15_spmd, %region_16.16_spmd} | conditional | flops 613941248 | bytes 20741160 | solution.py:223
  290.4 3.7 fusion.91
  294.2 6.4 fusion.29
  304.7 11.8 %conditional.7 = (f32[256,12,64]{0,2,1:T(8,128)}) conditional(s32[]{:T(128)} %convert_element_type.315, f32[256,12,64]{0,2,1:T(8,128)} %get-tuple-element.1570, (s32[256]{0:T(256)}, s32[512]{0:T(512)S(1)}, bf16[2048,768]{0,1:T(8,128)(2,1)}, s32[]{:T(128)}, bf16[256,12,64]{0,2,1:T(8,128)(2,1)S(1)}, /*index=5*/f32[12,256]{1,0:T(8,128)}, ...), branch_computations={%region_15.15_spmd, %region_16.16_spmd} | conditional | flops 613941248 | bytes 20741160 | solution.py:223
  306.2 3.7 fusion.91
  310.0 6.4 fusion.29
  320.5 11.8 %conditional.7 = (f32[256,12,64]{0,2,1:T(8,128)}) conditional(s32[]{:T(128)} %convert_element_type.315, f32[256,12,64]{0,2,1:T(8,128)} %get-tuple-element.1570, (s32[256]{0:T(256)}, s32[512]{0:T(512)S(1)}, bf16[2048,768]{0,1:T(8,128)(2,1)}, s32[]{:T(128)}, bf16[256,12,64]{0,2,1:T(8,128)(2,1)S(1)}, /*index=5*/f32[12,256]{1,0:T(8,128)}, ...), branch_computations={%region_15.15_spmd, %region_16.16_spmd} | conditional | flops 613941248 | bytes 20741160 | solution.py:223
  322.0 3.7 fusion.91
  325.8 6.4 fusion.29
  336.4 4.6 copy.80
  342.9 66.5 %while.50 = (s32[]{:T(128)}, f32[256,12,64]{0,2,1:T(8,128)}, f32[256,12,64]{0,2,1:T(8,128)}, s32[2048]{0:T(1024)}, s32[]{:T(128)}, /*index=5*/s32[]{:T(128)}, s3...) while((s32[]{:T(128)}, f32[256,12,64]{0,2,1:T(8,128)}, ...), condition=%wide.region_21.22_spmd, body=%wide.region_18.21_spmd.sunk | while | flops 821755904 | bytes 29670792 | solution.py:275
  346.9 16.9 %conditional.8 = ((f32[256,12,64]{0,2,1:T(8,128)}, f32[256,12,64]{0,2,1:T(8,128)})) conditional(s32[]{:T(128)} %convert_element_type.316, (f32[256,12,64]{0,2,1:T(8,128)}, f32[256,12,64]{0,2,1:T(8,128)}) %tuple.174, (s32[512]{0:T(512)S(1)}, s32[256]{0:T(256)S(1)}, bf16[2048,768]{0,1:T(8,128)(2,1)}, s32[]{:T(128)}, ...), branch_computations={%region_19.19_spmd, %region_20.20_spmd} | conditional | flops 821755904 | bytes 29666336 | solution.py:273
  348.4 3.7 fusion.92
  352.2 6.7 fusion.50
  358.9 4.9 fusion.45
  367.7 16.9 %conditional.8 = ((f32[256,12,64]{0,2,1:T(8,128)}, f32[256,12,64]{0,2,1:T(8,128)})) conditional(s32[]{:T(128)} %convert_element_type.316, (f32[256,12,64]{0,2,1:T(8,128)}, f32[256,12,64]{0,2,1:T(8,128)}) %tuple.174, (s32[512]{0:T(512)S(1)}, s32[256]{0:T(256)S(1)}, bf16[2048,768]{0,1:T(8,128)(2,1)}, s32[]{:T(128)}, ...), branch_computations={%region_19.19_spmd, %region_20.20_spmd} | conditional | flops 821755904 | bytes 29666336 | solution.py:273
  369.2 3.7 fusion.92
  373.1 6.7 fusion.50
  379.8 4.9 fusion.45
  388.6 16.9 %conditional.8 = ((f32[256,12,64]{0,2,1:T(8,128)}, f32[256,12,64]{0,2,1:T(8,128)})) conditional(s32[]{:T(128)} %convert_element_type.316, (f32[256,12,64]{0,2,1:T(8,128)}, f32[256,12,64]{0,2,1:T(8,128)}) %tuple.174, (s32[512]{0:T(512)S(1)}, s32[256]{0:T(256)S(1)}, bf16[2048,768]{0,1:T(8,128)(2,1)}, s32[]{:T(128)}, ...), branch_computations={%region_19.19_spmd, %region_20.20_spmd} | conditional | flops 821755904 | bytes 29666336 | solution.py:273
  390.1 3.7 fusion.92
  393.9 6.7 fusion.50
  400.6 4.9 fusion.45
  410.7 2.9 fusion.84
  413.6 2.8 fusion.55
  416.4 5.8 copy.92
  425.4 5.1 convolution_convert_fusion.1
  431.6 5.1 convolution_convert_fusion
  440.5 58.1 %reduce-scatter.16.cloned.1.call-done = bf16[96,2304]{1,0:T(8,128)(2,1)} async-done(((bf16[768,2304]{1,0:T(8,128)(2,1)}), bf16[96,2304]{1,0:T(8,128)(2,1)}) %reduce-scatter.16.cloned.1.call-update) | async-done | bytes 442384
  498.7 2.1 copy.93
  500.8 38.3 %reduce-scatter.10.cloned.1.call-done = bf16[96,768]{1,0:T(8,128)(2,1)} async-done(((bf16[768,768]{1,0:T(8,128)(2,1)}), bf16[96,768]{1,0:T(8,128)(2,1)}) %reduce-scatter.10.cloned.1.call-update) | async-done | bytes 147472 | tf_op jit(solution)/shard_map/reduce_scatter | solution.py:308
  539.1 57.3 %reduce-scatter.12.cloned.1.call-done = bf16[96,3072]{1,0:T(8,128)(2,1)} async-done(((bf16[768,3072]{1,0:T(8,128)(2,1)}), bf16[96,3072]{1,0:T(8,128)(2,1)}) %reduce-scatter.12.cloned.1.call-update) | async-done | bytes 589840 | tf_op jit(solution)/shard_map/reduce_scatter | solution.py:320
  596.3 57.1 %reduce-scatter.14.cloned.1.call-done = bf16[384,768]{1,0:T(8,128)(2,1)} async-done(((bf16[3072,768]{1,0:T(8,128)(2,1)}), bf16[384,768]{1,0:T(8,128)(2,1)}) %reduce-scatter.14.cloned.1.call-update) | async-done | bytes 589840 | tf_op jit(solution)/shard_map/reduce_scatter | solution.py:326
  658.2 23.6 %all-reduce.13 = (bf16[768]{0:T(1024)(128)(2,1)S(1)}, bf16[768]{0:T(1024)(128)(2,1)S(1)}, bf16[768]{0:T(1024)(128)(2,1)S(1)}, bf16[768]{0:T(1024)(128)(2,1)S(1)}...) all-reduce(bf16[768]{0:T(1024)(128)(2,1)} %dynamic-update-slice.5, ...), channel_id=1, replica_groups=mesh['shard'=8,'replica'=4] {'shard'}, use_global_device_ids=true, to_apply=%add.5 | all-reduce | flops 8448 | bytes 33792
  683.9 4.0 convolution_add_fusion.2
  687.9 2.8 reduce-scatter.18.cloned.1.call-done
  691.5 11.9 %all-reduce.15 = (bf16[2,96]{1,0:T(2,128)(2,1)S(1)}, bf16[96]{0:T(256)(128)(2,1)S(1)}, bf16[96]{0:T(256)(128)(2,1)S(1)}, bf16[96]{0:T(256)(128)(2,1)S(1)}, bf16[...) all-reduce(bf16[2,96]{1,0:T(2,128)(2,1)S(1)} %copy.95, ...), channel_id=1, replica_groups=mesh['shard'=8,'replica'=4] {'replica'}, use_global_device_ids=true, to_apply=%region_27.28 | all-reduce | flops 1152 | bytes 4608 | tf_op jit(solution)/shard_map/psum | solution.py:341
  707.7 66.8 %all-reduce.19.cloned.1.call-done = (bf16[96,2304]{0,1:T(8,128)(2,1)}, bf16[96,768]{1,0:T(8,128)(2,1)}, bf16[96,3072]{1,0:T(8,128)(2,1)}, bf16[384,768]{1,0:T(8,128)(2,1)}) async-done(((bf16[96,2304]{0,1:T(8,128)(2,1)}, bf16[96,768]{1,0:T(8,128)(2,1)}, bf16[96,3072]{1,0:T(8,128)(2,1)}, bf16[384,768]{1,0:T(8,128)(2,1)}), (bf16[96,2304]{0,1:T(8,128)(2,1)}, bf16[96,768]{1,0:T(8,128)(2,1)}, ...) | async-done | bytes 1769488 | tf_op jit(solution)/shard_map/psum | solution.py:340
  774.5 2.3 copy.81
  778.4 2.2 convert_element_type.234
  (293 shorter events, 88.8 us)
Async XLA Ops:
  7.2 39.3 %all-gather.12.cloned.1.call-start = ((), (), s32[]{:S(2)}) async-start(), calls=%async_computation.5 | async-start | bytes 3981312 | tf_op jit(solution)/shard_map/all_gather | solution.py:74
  7.9 42.7 %copy-start.42 = (bf16[2,96]{1,0:T(2,128)(2,1)S(1)}, bf16[2,96]{1,0:T(2,128)(2,1)}, u32[]{:S(2)}) copy-start(bf16[2,96]{1,0:T(2,128)(2,1)} %param.30) | copy-start | bytes 1156
  7.9 99.1 %all-gather.14.cloned.1.call-start = ((), (), s32[]{:S(2)}) async-start(), calls=%async_computation.6 | async-start | bytes 3538944 | tf_op jit(solution)/shard_map/all_gather | solution.py:94
  49.7 12.5 %copy-start.40 = (u32[32]{0:T(128)S(1)}, u32[32]{0:T(128)}, u32[]{:S(2)}) copy-start(u32[32]{0:T(128)} %constant.230) | copy-start | bytes 388
  49.7 13.8 %copy-start.43 = (bf16[96]{0:T(256)(128)(2,1)S(1)}, bf16[96]{0:T(256)(128)(2,1)}, u32[]{:S(2)}) copy-start(bf16[96]{0:T(256)(128)(2,1)} %param.32) | copy-start | bytes 580
  49.7 14.0 %copy-start.44 = (bf16[96]{0:T(256)(128)(2,1)S(1)}, bf16[96]{0:T(256)(128)(2,1)}, u32[]{:S(2)}) copy-start(bf16[96]{0:T(256)(128)(2,1)} %param.34) | copy-start | bytes 580
  49.7 14.2 %copy-start.45 = (bf16[96]{0:T(256)(128)(2,1)S(1)}, bf16[96]{0:T(256)(128)(2,1)}, u32[]{:S(2)}) copy-start(bf16[96]{0:T(256)(128)(2,1)} %param.33) | copy-start | bytes 580
  49.7 14.4 %copy-start.46 = (bf16[96]{0:T(256)(128)(2,1)S(1)}, bf16[96]{0:T(256)(128)(2,1)}, u32[]{:S(2)}) copy-start(bf16[96]{0:T(256)(128)(2,1)} %param.38) | copy-start | bytes 580
  49.8 14.7 %copy-start.47 = (bf16[96]{0:T(256)(128)(2,1)S(1)}, bf16[96]{0:T(256)(128)(2,1)}, u32[]{:S(2)}) copy-start(bf16[96]{0:T(256)(128)(2,1)} %param.39) | copy-start | bytes 580
  49.8 39.1 %copy-start.41 = (bf16[384]{0:T(512)(128)(2,1)S(1)}, bf16[384]{0:T(512)(128)(2,1)}, u32[]{:S(2)}) copy-start(bf16[384]{0:T(512)(128)(2,1)} %param.36) | copy-start | bytes 2308
  49.8 47.2 %copy-start.20 = (s32[256]{0:T(256)S(1)}, s32[256]{0:T(256)}, u32[]{:S(2)}) copy-start(s32[256]{0:T(256)} %param.28) | copy-start | bytes 3076
  50.6 67.2 %all-gather.16.cloned.1.call-start = ((), (), s32[]{:S(2)}) async-start(), calls=%async_computation.7 | async-start | bytes 3538944 | tf_op jit(solution)/shard_map/all_gather | solution.py:95
  60.4 46.3 %copy-start.7 = (bf16[256,768]{1,0:T(8,128)(2,1)}, bf16[256,768]{1,0:T(8,128)(2,1)S(1)}, u32[]{:S(2)}) copy-start(bf16[256,768]{1,0:T(8,128)(2,1)S(1)} %get-tuple-element.1236) | copy-start | bytes 1179652
  60.4 95.2 %all-gather.18.cloned.1.call-start = ((), (), s32[]{:S(2)}) async-start(), calls=%async_computation.8 | async-start | bytes 1327104 | tf_op jit(solution)/shard_map/all_gather | solution.py:75
  61.0 123.0 %all-gather.20.cloned.1.call-start = ((), (), s32[]{:S(2)}) async-start(), calls=%async_computation.9 | async-start | bytes 5308416 | tf_op jit(solution)/shard_map/all_gather | solution.py:143
  61.6 163.0 %all-gather.22.cloned.1.call-start = ((), (), s32[]{:S(2)}) async-start(), calls=%async_computation.10 | async-start | bytes 5308416 | tf_op jit(solution)/shard_map/all_gather | solution.py:145
  62.2 196.5 %all-gather.24.cloned.1.call-start = ((), (), s32[]{:S(2)}) async-start(), calls=%async_computation.11 | async-start | bytes 3538944 | tf_op jit(solution)/shard_map/all_gather | solution.py:230
  97.0 127.6 %copy-start.25 = (f32[768]{0:T(1024)}, f32[768]{0:T(1024)S(1)}, u32[]{:S(2)}) copy-start(f32[768]{0:T(1024)S(1)} %convert_element_type.209) | copy-start | bytes 9220
  97.0 139.6 %copy-start.23 = (f32[768]{0:T(1024)}, f32[768]{0:T(1024)S(1)}, u32[]{:S(2)}) copy-start(f32[768]{0:T(1024)S(1)} %convert_element_type.208) | copy-start | bytes 9220
  97.0 133.3 %copy-start.27 = (f32[768]{0:T(1024)}, f32[768]{0:T(1024)S(1)}, u32[]{:S(2)}) copy-start(f32[768]{0:T(1024)S(1)} %convert_element_type.214) | copy-start | bytes 9220
  106.7 229.7 %all-gather.26.cloned.1.call-start = ((), (), s32[]{:S(2)}) async-start(), calls=%async_computation.12 | async-start | bytes 3538944 | tf_op jit(solution)/shard_map/all_gather | solution.py:231
  122.6 33.5 %copy-start.12 = (bf16[256,768]{1,0:T(8,128)(2,1)S(1)}, bf16[256,768]{1,0:T(8,128)(2,1)}, u32[]{:S(2)}) copy-start(bf16[256,768]{1,0:T(8,128)(2,1)} %param.27) | copy-start | bytes 1179652
  155.6 40.5 %copy-start.9 = (bf16[256,12,64]{0,2,1:T(8,128)(2,1)}, bf16[256,12,64]{0,2,1:T(8,128)(2,1)S(1)}, u32[]{:S(2)}) copy-start(bf16[256,12,64]{0,2,1:T(8,128)(2,1)S(1)} %fusion.70) | copy-start | bytes 1179652
  158.0 78.6 %copy-start.31 = (f32[256]{0:T(256)}, f32[256]{0:T(256)S(1)}, u32[]{:S(2)}) copy-start(f32[256]{0:T(256)S(1)} %broadcast_multiply_fusion.1) | copy-start | bytes 3076
  158.3 78.4 %copy-start.36 = (f32[256]{0:T(256)}, f32[256]{0:T(256)S(1)}, u32[]{:S(2)}) copy-start(f32[256]{0:T(256)S(1)} %fusion.71) | copy-start | bytes 3076
  224.6 6.1 slice-start.2
  224.6 4.7 copy-start.11
  224.6 6.1 slice-start.3
  224.6 6.1 copy-start.49
  229.1 5.2 copy-start
  229.1 2.4 copy-start.48
  229.1 5.2 copy-start.29
  229.3 4.9 copy-start.35
  230.3 4.0 slice-start
  230.6 3.6 copy-start.4
  230.7 3.6 copy-start.38
  231.5 2.8 slice-start.1
  234.3 2.3 copy-start.14
  234.3 2.7 copy-start.6
  236.6 3.0 copy-start.8
  237.0 26.5 %copy-start.2 = (f32[256,768]{1,0:T(8,128)}, f32[256,768]{1,0:T(8,128)S(1)}, u32[]{:S(2)}) copy-start(f32[256,768]{1,0:T(8,128)S(1)} %get-tuple-element.1214) | copy-start | bytes 2359300
  237.0 1.4 copy-start.33
  238.3 260.4 %reduce-scatter.16.cloned.1.call-start = ((), (), s32[]{:S(2)}) async-start(), calls=%async_computation.16 | async-start | bytes 3981312
  242.4 21.0 %copy-start.16 = (f32[12,256]{1,0:T(8,128)S(1)}, f32[12,256]{1,0:T(8,128)}, u32[]{:S(2)}) copy-start(f32[12,256]{1,0:T(8,128)} %copy-done.15) | copy-start | bytes 36868
  290.4 3.7 copy-start.21
  306.2 3.7 copy-start.21
  322.0 3.7 copy-start.21
  336.3 6.6 copy-start.22
  409.4 4.2 copy-start.13
  410.7 2.9 copy-start.18
  422.2 3.1 copy-start.24
  422.3 3.1 copy-start.26
  422.3 3.1 copy-start.32
  422.3 3.1 copy-start.37
  422.3 116.8 %reduce-scatter.10.cloned.1.call-start = ((), (), s32[]{:S(2)}) async-start(), calls=%async_computation.13 | async-start | bytes 1327104 | tf_op jit(solution)/shard_map/reduce_scatter | solution.py:308
  425.1 171.3 %reduce-scatter.12.cloned.1.call-start = ((), (), s32[]{:S(2)}) async-start(), calls=%async_computation.14 | async-start | bytes 5308416 | tf_op jit(solution)/shard_map/reduce_scatter | solution.py:320
  430.5 222.9 %reduce-scatter.14.cloned.1.call-start = ((), (), s32[]{:S(2)}) async-start(), calls=%async_computation.15 | async-start | bytes 5308416 | tf_op jit(solution)/shard_map/reduce_scatter | solution.py:326
  436.7 245.6 %copy-start.1 = (f32[256,768]{1,0:T(8,128)S(1)}, f32[256,768]{1,0:T(8,128)}, u32[]{:S(2)}) copy-start(f32[256,768]{1,0:T(8,128)} %copy-done) | copy-start | bytes 2359300
  436.7 245.6 %copy-start.28 = (f32[768]{0:T(1024)S(1)}, f32[768]{0:T(1024)}, u32[]{:S(2)}) copy-start(f32[768]{0:T(1024)} %copy-done.27) | copy-start | bytes 9220
  436.8 245.6 %copy-start.30 = (f32[256]{0:T(256)S(1)}, f32[256]{0:T(256)}, u32[]{:S(2)}) copy-start(f32[256]{0:T(256)} %copy-done.29) | copy-start | bytes 3076
  436.8 247.1 %copy-start.19 = (bf16[256,12,64]{0,2,1:T(8,128)(2,1)S(1)}, bf16[256,12,64]{0,2,1:T(8,128)(2,1)}, u32[]{:S(2)}) copy-start(bf16[256,12,64]{0,2,1:T(8,128)(2,1)} %copy-done.18) | copy-start | bytes 1179652
  436.8 254.0 %reduce-scatter.18.cloned.1.call-start = ((), (), s32[]{:S(2)}) async-start(), calls=%async_computation.17 | async-start | bytes 221184
  440.5 334.0 %all-reduce.19.cloned.1.call-start = ((), (), s32[]{:S(2)}) async-start(), calls=%async_computation.18 | async-start | bytes 3833856 | tf_op jit(solution)/shard_map/psum | solution.py:340
  774.5 6.1 copy-start.17
  (6 other events, 6.5 us)
Sparse Core Ops, SparseCore 0:
  9.9 36.5 all-gather.11
  50.7 32.3 all-gather.13
  85.6 32.1 all-gather.15
  119.5 23.9 all-gather.17
  145.2 38.7 all-gather.19
  185.8 38.7 all-gather.21
  226.5 32.1 all-gather.23
  260.6 32.3 all-gather.25
  422.4 76.2 reduce-scatter.15
  502.3 36.6 reduce-scatter.9
  542.5 53.7 reduce-scatter.11
  599.6 53.7 reduce-scatter.13
  657.1 33.6 reduce-scatter.17
  693.8 80.6 all-reduce.18
where the time goes:
time: 794 us; the launch traced here: 788 us
  waiting for transfers between devices  398 us (50%)
  matrix products  130 us (16%)
  blocking collectives  103 us (13%)
  local copies, waits for them, and re-layouts  79.1 us (10%)
  loops' own time  32.1 us (4%)
  other arithmetic  27.6 us (3%)
  between operations  16.9 us (2%)
    psum x1, waiting for transfers between devices, body(): lax.psum(shard_grads[0].astype(jnp.bfloat16), 'replica').astype(jnp.float32)  66.8 us
    unnamed x16, waiting for transfers between devices  63.4 us
    reduce_scatter x1, waiting for transfers between devices, body(): lax.psum_scatter(local_grads[6].astype(jnp.bfloat16), 'shard', scatter_di...  57.3 us
    reduce_scatter x1, waiting for transfers between devices, body(): lax.psum_scatter(local_grads[8].astype(jnp.bfloat16), 'shard', scatter_di...  57.1 us
    unnamed x2, blocking collectives  47.7 us
    all_gather x1, waiting for transfers between devices, body(): lax.all_gather(w_qkv, 'shard', axis=0, tiled=True)  38.5 us
    reduce_scatter x1, waiting for transfers between devices, body(): lax.psum_scatter(local_grads[2].astype(jnp.bfloat16), 'shard', scatter_di...  38.3 us
    all_gather x1, waiting for transfers between devices, body(): lax.all_gather(w_back, 'shard', axis=0, tiled=True)  28.4 us
  transfers between devices with their start and end apart: 14, of which 11 were waited for; matrix products, arithmetic and copies ran while one was open for 19% of the time, Pallas kernels for 0%

commit v1 on v0

--- a/solution.py
+++ b/solution.py
@@ -227,8 +227,14 @@
         lax.all_gather(log_total, "shard", axis=1, tiled=True),
         lax.all_gather(delta, "shard", axis=1, tiled=True),
     )
-    query_piece = lax.all_gather(query, "shard", axis=0, tiled=True)
-    dctx_piece = lax.all_gather(d_context, "shard", axis=0, tiled=True)
+    results_pass = lambda inputs, original, dev_axis: jnp.split(
+        lax.all_gather(
+            jnp.concatenate([inputs, original], axis=1), tiled=True, axis_name=dev_axis, axis=0
+        ),
+        [inputs.shape[1]],
+        axis=1,
+    )
+    query_piece, dctx_piece = results_pass(query, d_context, "shard")
     key_seg_piece = lax.all_gather(segment_ids, "shard", axis=0, tiled=True)
     count = query_piece.shape[0]
     key_block = block_size(count)

time: 794 us -> 786 us (0.990)
  waiting for transfers between devices: 398 us -> 385 us
    all_gather x2 -> x1, waiting for transfers between devices: 16.3 us -> 0.02 us  [body(): lax.all_gather(jnp.concatenate([inputs, original], axis=1), tiled=True, a...]
    unnamed x16 -> x15, waiting for transfers between devices: 63.4 us -> 63.3 us
  transfers between devices with their start and end apart: 14 -> 13, of which waited for: 11 -> 10; matrix products, arithmetic and copies ran while one was open for 19% -> 16% of each run, Pallas kernels for 0% -> 0%
where the time goes in v1:
time: 786 us; the launch traced here: 781 us
  waiting for transfers between devices  385 us (49%)
  matrix products  130 us (17%)
  blocking collectives  104 us (13%)
  local copies, waits for them, and re-layouts  82.7 us (11%)
  loops' own time  31.8 us (4%)
  other arithmetic  29.4 us (4%)
  between operations  16.9 us (2%)
    psum x1, waiting for transfers between devices, body(): lax.psum(shard_grads[0].astype(jnp.bfloat16), 'replica').astype(jnp.float32)  66.9 us
    unnamed x15, waiting for transfers between devices  63.3 us
    reduce_scatter x1, waiting for transfers between devices, body(): lax.psum_scatter(local_grads[8].astype(jnp.bfloat16), 'shard', scatter_di...  57.3 us
    reduce_scatter x1, waiting for transfers between devices, body(): lax.psum_scatter(local_grads[6].astype(jnp.bfloat16), 'shard', scatter_di...  57.1 us
    unnamed x2, blocking collectives  47.8 us
    all_gather x1, waiting for transfers between devices, body(): lax.all_gather(w_qkv, 'shard', axis=0, tiled=True)  38.5 us
    reduce_scatter x1, waiting for transfers between devices, body(): lax.psum_scatter(local_grads[2].astype(jnp.bfloat16), 'shard', scatter_di...  38.5 us
    all_gather x1, waiting for transfers between devices, body(): lax.all_gather(w_in, 'shard', axis=0, tiled=True)  28.8 us
  transfers between devices with their start and end apart: 13, of which 10 were waited for; matrix products, arithmetic and copies ran while one was open for 16% of the time, Pallas kernels for 0%

profile of v1, /device:TPU:0, one launch (start us, length us, event | category | flops | bytes accessed | tf_op | source)
XLA Modules:
  0.0 780.5 jit_solution(13380063827824222608)
XLA Ops:
  8.0 38.5 %all-gather.11.cloned.1.call-done = bf16[768,2304]{1,0:T(8,128)(2,1)} async-done(((bf16[96,2304]{1,0:T(8,128)(2,1)}), bf16[768,2304]{1,0:T(8,128)(2,1)}) %all-gather.11.cloned.1.call-update) | async-done | bytes 3538960 | tf_op jit(solution)/shard_map/all_gather | solution.py:74
  46.5 3.2 fusion.94
  50.7 8.7 %all-gather.1 = bf16[8,96,2]{1,2,0:T(2,128)(2,1)S(1)} all-gather(bf16[1,96,2]{1,2,0:T(2,128)(2,1)S(1)} %bitcast.173), channel_id=1, replica_groups=mesh['shard'=8,'replica'=4] {'shard'}, dimensions={0}, use_global_device_ids=true | all-gather | bytes 3456 | tf_op jit(solution)/shard_map/all_gather | solution.py:76
  64.7 24.2 %all-reduce.14 = (bf16[768]{0:T(1024)(128)(2,1)S(1)}, bf16[768]{0:T(1024)(128)(2,1)S(1)}, bf16[768]{0:T(1024)(128)(2,1)S(1)}, bf16[768]{0:T(1024)(128)(2,1)S(1)}, bf16[768]{0:T(1024)(128)(2,1)S(1)}) all-reduce(bf16[768]{0:T(1024)(128)(2,1)S(1)} %dynamic-update-slice, ...), channel_id=1, replica_groups=mesh['shard'=8,'replica'=4] {'shard'}, use_global_device_ids=true, to_apply=%add | all-reduce | flops 3840 | bytes 15360
  88.8 8.1 %all-gather.2 = bf16[8,1,384]{2,1,0:T(2,128)(2,1)S(1)} all-gather(bf16[1,1,384]{2,1,0:T(2,128)(2,1)S(1)} %reshape.302), channel_id=1, replica_groups=mesh['shard'=8,'replica'=4] {'shard'}, dimensions={0}, use_global_device_ids=true | all-gather | bytes 6912 | tf_op jit(solution)/shard_map/all_gather | solution.py:144
  97.0 9.1 %all-gather = s32[8,1,256]{2,1,0:T(1,128)S(1)} all-gather(s32[1,1,256]{2,1,0:T(1,128)S(1)} %bitcast.168), channel_id=1, replica_groups=mesh['shard'=8,'replica'=4] {'shard'}, dimensions={0}, use_global_device_ids=true | all-gather | bytes 9216 | tf_op jit(solution)/shard_map/all_gather | solution.py:96
  106.9 4.8 copy.72
  111.7 6.1 all-gather.15.cloned.1.call-done
  117.8 4.7 copy.73
  122.6 30.1 %while.48 = (s32[]{:T(128)}, f32[12,256]{1,0:T(8,128)S(1)}, f32[12,256]{1,0:T(8,128)S(1)}, f32[256,12,64]{0,2,1:T(8,128)S(1)}, s32[2048]{0:T(1024)S(1)}, /*index...) while((s32[]{:T(128)}, f32[12,256]{1,0:T(8,128)S(1)}, ...), condition=%wide.region_5.6_spmd, body=%wide.region_0.5_spmd.sunk | while | flops 420488192 | bytes 26287476 | solution.py:130
  125.9 5.7 conditional.6
  134.8 5.6 conditional.6
  143.7 5.6 conditional.6
  152.9 2.1 fusion.89
  155.2 28.8 %all-gather.19.cloned.1.call-done = bf16[768,3072]{1,0:T(8,128)(2,1)} async-done(((bf16[96,3072]{1,0:T(8,128)(2,1)}), bf16[768,3072]{1,0:T(8,128)(2,1)}) %all-gather.19.cloned.1.call-update) | async-done | bytes 4718608 | tf_op jit(solution)/shard_map/all_gather | solution.py:143
  184.0 12.1 %multiply_convert_fusion.8 = (bf16[256,3072]{1,0:T(8,128)(2,1)}, f32[256,3072]{1,0:T(8,128)}, f32[256,3072]{1,0:T(8,128)}) fusion(f32[3072]{0:T(1024)S(1)} %bitcast.172, bf16[768,3072]{1,0:T(8,128)(2,1)} %all-gather.19.cloned.1.call-done, f32[256,768]{1,0:T(8,128)S(1)} %get-tuple-element.1248, f32[768]{0:T(1024)S(1)} %convert_element_type.209, ...), kind=kOutput, calls=%fused_computation.63 | convolution fusion | flops 1260847104 | bytes 13389824 | tf_op jit(solution)/shard_map/dot_general | solution.py:151
  196.2 28.4 %all-gather.21.cloned.1.call-done = bf16[3072,768]{1,0:T(8,128)(2,1)} async-done(((bf16[384,768]{1,0:T(8,128)(2,1)}), bf16[3072,768]{1,0:T(8,128)(2,1)}) %all-gather.21.cloned.1.call-update) | async-done | bytes 4718608 | tf_op jit(solution)/shard_map/all_gather | solution.py:145
  224.6 4.5 fusion.90
  231.5 2.8 fusion.91
  234.4 2.2 multiply_reduce_fusion.1
  245.0 9.6 %all_gather.74 = f32[12,2048]{1,0:T(8,128)S(1)} all-gather(f32[12,256]{1,0:T(8,128)} %log_add_fusion), channel_id=1, replica_groups=mesh['shard'=8,'replica'=4] {'shard'}, dimensions={1}, use_global_device_ids=true | all-gather | bytes 110592 | tf_op jit(solution)/shard_map/all_gather | solution.py:227
  256.3 8.4 %all_gather.75 = f32[12,2048]{1,0:T(8,128)S(1)} all-gather(f32[12,256]{1,0:T(8,128)} %fusion.66), channel_id=1, replica_groups=mesh['shard'=8,'replica'=4] {'shard'}, dimensions={1}, use_global_device_ids=true | all-gather | bytes 110592 | tf_op jit(solution)/shard_map/all_gather | solution.py:228
  265.7 51.1 %while.49 = (s32[]{:T(128)}, f32[256,12,64]{0,2,1:T(8,128)}, s32[2048]{0:T(1024)}, s32[]{:T(128)}, s32[]{:T(128)}, /*index=5*/s32[256]{0:T(256)}, bf16[2048,768]...) while((s32[]{:T(128)}, f32[256,12,64]{0,2,1:T(8,128)}, ...), condition=%wide.region_17.18_spmd, body=%wide.region_14.17_spmd.sunk | while | flops 613941248 | bytes 20745584 | solution.py:225
  269.8 11.8 %conditional.7 = (f32[256,12,64]{0,2,1:T(8,128)}) conditional(s32[]{:T(128)} %convert_element_type.315, f32[256,12,64]{0,2,1:T(8,128)} %get-tuple-element.1572, (s32[256]{0:T(256)}, s32[512]{0:T(512)S(1)}, bf16[2048,768]{0,1:T(8,128)(2,1)}, s32[]{:T(128)}, bf16[256,12,64]{0,2,1:T(8,128)(2,1)S(1)}, /*index=5*/f32[12,256]{1,0:T(8,128)}, ...), branch_computations={%region_15.15_spmd, %region_16.16_spmd} | conditional | flops 613941248 | bytes 20741160 | solution.py:223
  271.3 3.7 fusion.92
  275.1 6.5 fusion.29
  285.5 11.8 %conditional.7 = (f32[256,12,64]{0,2,1:T(8,128)}) conditional(s32[]{:T(128)} %convert_element_type.315, f32[256,12,64]{0,2,1:T(8,128)} %get-tuple-element.1572, (s32[256]{0:T(256)}, s32[512]{0:T(512)S(1)}, bf16[2048,768]{0,1:T(8,128)(2,1)}, s32[]{:T(128)}, bf16[256,12,64]{0,2,1:T(8,128)(2,1)S(1)}, /*index=5*/f32[12,256]{1,0:T(8,128)}, ...), branch_computations={%region_15.15_spmd, %region_16.16_spmd} | conditional | flops 613941248 | bytes 20741160 | solution.py:223
  287.0 3.7 fusion.92
  290.8 6.4 fusion.29
  301.1 11.8 %conditional.7 = (f32[256,12,64]{0,2,1:T(8,128)}) conditional(s32[]{:T(128)} %convert_element_type.315, f32[256,12,64]{0,2,1:T(8,128)} %get-tuple-element.1572, (s32[256]{0:T(256)}, s32[512]{0:T(512)S(1)}, bf16[2048,768]{0,1:T(8,128)(2,1)}, s32[]{:T(128)}, bf16[256,12,64]{0,2,1:T(8,128)(2,1)S(1)}, /*index=5*/f32[12,256]{1,0:T(8,128)}, ...), branch_computations={%region_15.15_spmd, %region_16.16_spmd} | conditional | flops 613941248 | bytes 20741160 | solution.py:223
  302.7 3.7 fusion.92
  306.5 6.4 fusion.29
  316.8 5.9 fusion.84
  322.7 4.7 copy.79
  327.5 4.7 copy.80
  334.3 66.9 %while.50 = (s32[]{:T(128)}, f32[256,12,64]{0,2,1:T(8,128)}, f32[256,12,64]{0,2,1:T(8,128)}, s32[2048]{0:T(1024)}, s32[]{:T(128)}, /*index=5*/s32[]{:T(128)}, s3...) while((s32[]{:T(128)}, f32[256,12,64]{0,2,1:T(8,128)}, ...), condition=%wide.region_21.22_spmd, body=%wide.region_18.21_spmd.sunk | while | flops 821755904 | bytes 29670792 | solution.py:281
  338.2 17.0 %conditional.8 = ((f32[256,12,64]{0,2,1:T(8,128)}, f32[256,12,64]{0,2,1:T(8,128)})) conditional(s32[]{:T(128)} %convert_element_type.316, (f32[256,12,64]{0,2,1:T(8,128)}, f32[256,12,64]{0,2,1:T(8,128)}) %tuple.175, (s32[512]{0:T(512)S(1)}, s32[256]{0:T(256)S(1)}, bf16[2048,768]{0,1:T(8,128)(2,1)}, s32[]{:T(128)}, ...), branch_computations={%region_19.19_spmd, %region_20.20_spmd} | conditional | flops 821755904 | bytes 29666336 | solution.py:279
  339.7 3.7 fusion.93
  343.6 6.8 fusion.50
  350.3 4.9 fusion.45
  359.2 17.0 %conditional.8 = ((f32[256,12,64]{0,2,1:T(8,128)}, f32[256,12,64]{0,2,1:T(8,128)})) conditional(s32[]{:T(128)} %convert_element_type.316, (f32[256,12,64]{0,2,1:T(8,128)}, f32[256,12,64]{0,2,1:T(8,128)}) %tuple.175, (s32[512]{0:T(512)S(1)}, s32[256]{0:T(256)S(1)}, bf16[2048,768]{0,1:T(8,128)(2,1)}, s32[]{:T(128)}, ...), branch_computations={%region_19.19_spmd, %region_20.20_spmd} | conditional | flops 821755904 | bytes 29666336 | solution.py:279
  360.7 3.7 fusion.93
  364.5 6.8 fusion.50
  371.3 4.9 fusion.45
  380.2 17.0 %conditional.8 = ((f32[256,12,64]{0,2,1:T(8,128)}, f32[256,12,64]{0,2,1:T(8,128)})) conditional(s32[]{:T(128)} %convert_element_type.316, (f32[256,12,64]{0,2,1:T(8,128)}, f32[256,12,64]{0,2,1:T(8,128)}) %tuple.175, (s32[512]{0:T(512)S(1)}, s32[256]{0:T(256)S(1)}, bf16[2048,768]{0,1:T(8,128)(2,1)}, s32[]{:T(128)}, ...), branch_computations={%region_19.19_spmd, %region_20.20_spmd} | conditional | flops 821755904 | bytes 29666336 | solution.py:279
  381.7 3.7 fusion.93
  385.5 6.8 fusion.50
  392.3 4.9 fusion.45
  402.4 2.9 fusion.85
  405.4 2.8 fusion.55
  408.2 5.8 copy.92
  417.1 5.1 convolution_convert_fusion.1
  423.4 5.1 convolution_convert_fusion
  432.3 58.4 %reduce-scatter.16.cloned.1.call-done = bf16[96,2304]{1,0:T(8,128)(2,1)} async-done(((bf16[768,2304]{1,0:T(8,128)(2,1)}), bf16[96,2304]{1,0:T(8,128)(2,1)}) %reduce-scatter.16.cloned.1.call-update) | async-done | bytes 442384
  492.7 38.5 %reduce-scatter.10.cloned.1.call-done = bf16[96,768]{1,0:T(8,128)(2,1)} async-done(((bf16[768,768]{1,0:T(8,128)(2,1)}), bf16[96,768]{1,0:T(8,128)(2,1)}) %reduce-scatter.10.cloned.1.call-update) | async-done | bytes 147472 | tf_op jit(solution)/shard_map/reduce_scatter | solution.py:314
  531.2 57.1 %reduce-scatter.12.cloned.1.call-done = bf16[96,3072]{1,0:T(8,128)(2,1)} async-done(((bf16[768,3072]{1,0:T(8,128)(2,1)}), bf16[96,3072]{1,0:T(8,128)(2,1)}) %reduce-scatter.12.cloned.1.call-update) | async-done | bytes 589840 | tf_op jit(solution)/shard_map/reduce_scatter | solution.py:326
  588.3 57.3 %reduce-scatter.14.cloned.1.call-done = bf16[384,768]{1,0:T(8,128)(2,1)} async-done(((bf16[3072,768]{1,0:T(8,128)(2,1)}), bf16[384,768]{1,0:T(8,128)(2,1)}) %reduce-scatter.14.cloned.1.call-update) | async-done | bytes 589840 | tf_op jit(solution)/shard_map/reduce_scatter | solution.py:332
  650.3 23.6 %all-reduce.13 = (bf16[768]{0:T(1024)(128)(2,1)S(1)}, bf16[768]{0:T(1024)(128)(2,1)S(1)}, bf16[768]{0:T(1024)(128)(2,1)S(1)}, bf16[768]{0:T(1024)(128)(2,1)S(1)}...) all-reduce(bf16[768]{0:T(1024)(128)(2,1)} %dynamic-update-slice.5, ...), channel_id=1, replica_groups=mesh['shard'=8,'replica'=4] {'shard'}, use_global_device_ids=true, to_apply=%add.5 | all-reduce | flops 8448 | bytes 33792
  676.1 4.0 convolution_add_fusion.2
  680.1 2.6 reduce-scatter.18.cloned.1.call-done
  683.5 12.0 %all-reduce.15 = (bf16[2,96]{1,0:T(2,128)(2,1)S(1)}, bf16[96]{0:T(256)(128)(2,1)S(1)}, bf16[96]{0:T(256)(128)(2,1)S(1)}, bf16[96]{0:T(256)(128)(2,1)S(1)}, bf16[...) all-reduce(bf16[2,96]{1,0:T(2,128)(2,1)S(1)} %copy.95, ...), channel_id=1, replica_groups=mesh['shard'=8,'replica'=4] {'replica'}, use_global_device_ids=true, to_apply=%region_27.28 | all-reduce | flops 1152 | bytes 4608 | tf_op jit(solution)/shard_map/psum | solution.py:347
  699.7 66.9 %all-reduce.19.cloned.1.call-done = (bf16[96,2304]{0,1:T(8,128)(2,1)}, bf16[96,768]{1,0:T(8,128)(2,1)}, bf16[96,3072]{1,0:T(8,128)(2,1)}, bf16[384,768]{1,0:T(8,128)(2,1)}) async-done(((bf16[96,2304]{0,1:T(8,128)(2,1)}, bf16[96,768]{1,0:T(8,128)(2,1)}, bf16[96,3072]{1,0:T(8,128)(2,1)}, bf16[384,768]{1,0:T(8,128)(2,1)}), (bf16[96,2304]{0,1:T(8,128)(2,1)}, bf16[96,768]{1,0:T(8,128)(2,1)}, ...) | async-done | bytes 1769488 | tf_op jit(solution)/shard_map/psum | solution.py:346
  766.6 2.3 copy.81
  770.5 2.2 convert_element_type.234
  (292 shorter events, 87.3 us)
Async XLA Ops:
  7.2 39.3 %all-gather.11.cloned.1.call-start = ((), (), s32[]{:S(2)}) async-start(), calls=%async_computation.5 | async-start | bytes 3981312 | tf_op jit(solution)/shard_map/all_gather | solution.py:74
  7.9 42.7 %copy-start.42 = (bf16[2,96]{1,0:T(2,128)(2,1)S(1)}, bf16[2,96]{1,0:T(2,128)(2,1)}, u32[]{:S(2)}) copy-start(bf16[2,96]{1,0:T(2,128)(2,1)} %param.30) | copy-start | bytes 1156
  7.9 99.0 %all-gather.13.cloned.1.call-start = ((), (), s32[]{:S(2)}) async-start(), calls=%async_computation.6 | async-start | bytes 3538944 | tf_op jit(solution)/shard_map/all_gather | solution.py:94
  49.7 12.5 %copy-start.40 = (u32[32]{0:T(128)S(1)}, u32[32]{0:T(128)}, u32[]{:S(2)}) copy-start(u32[32]{0:T(128)} %constant.230) | copy-start | bytes 388
  49.7 13.8 %copy-start.43 = (bf16[96]{0:T(256)(128)(2,1)S(1)}, bf16[96]{0:T(256)(128)(2,1)}, u32[]{:S(2)}) copy-start(bf16[96]{0:T(256)(128)(2,1)} %param.32) | copy-start | bytes 580
  49.7 14.0 %copy-start.44 = (bf16[96]{0:T(256)(128)(2,1)S(1)}, bf16[96]{0:T(256)(128)(2,1)}, u32[]{:S(2)}) copy-start(bf16[96]{0:T(256)(128)(2,1)} %param.34) | copy-start | bytes 580
  49.7 14.2 %copy-start.45 = (bf16[96]{0:T(256)(128)(2,1)S(1)}, bf16[96]{0:T(256)(128)(2,1)}, u32[]{:S(2)}) copy-start(bf16[96]{0:T(256)(128)(2,1)} %param.33) | copy-start | bytes 580
  49.7 14.4 %copy-start.46 = (bf16[96]{0:T(256)(128)(2,1)S(1)}, bf16[96]{0:T(256)(128)(2,1)}, u32[]{:S(2)}) copy-start(bf16[96]{0:T(256)(128)(2,1)} %param.38) | copy-start | bytes 580
  49.8 14.7 %copy-start.47 = (bf16[96]{0:T(256)(128)(2,1)S(1)}, bf16[96]{0:T(256)(128)(2,1)}, u32[]{:S(2)}) copy-start(bf16[96]{0:T(256)(128)(2,1)} %param.39) | copy-start | bytes 580
  49.8 39.1 %copy-start.41 = (bf16[384]{0:T(512)(128)(2,1)S(1)}, bf16[384]{0:T(512)(128)(2,1)}, u32[]{:S(2)}) copy-start(bf16[384]{0:T(512)(128)(2,1)} %param.36) | copy-start | bytes 2308
  49.8 47.2 %copy-start.19 = (s32[256]{0:T(256)S(1)}, s32[256]{0:T(256)}, u32[]{:S(2)}) copy-start(s32[256]{0:T(256)} %param.28) | copy-start | bytes 3076
  50.6 67.2 %all-gather.15.cloned.1.call-start = ((), (), s32[]{:S(2)}) async-start(), calls=%async_computation.7 | async-start | bytes 3538944 | tf_op jit(solution)/shard_map/all_gather | solution.py:95
  60.4 92.4 %all-gather.17.cloned.1.call-start = ((), (), s32[]{:S(2)}) async-start(), calls=%async_computation.8 | async-start | bytes 1327104 | tf_op jit(solution)/shard_map/all_gather | solution.py:75
  61.0 123.0 %all-gather.19.cloned.1.call-start = ((), (), s32[]{:S(2)}) async-start(), calls=%async_computation.9 | async-start | bytes 5308416 | tf_op jit(solution)/shard_map/all_gather | solution.py:143
  61.6 163.0 %all-gather.21.cloned.1.call-start = ((), (), s32[]{:S(2)}) async-start(), calls=%async_computation.10 | async-start | bytes 5308416 | tf_op jit(solution)/shard_map/all_gather | solution.py:145
  62.1 254.7 %all-gather.23.cloned.1.call-start = ((), (), s32[]{:S(2)}) async-start(), calls=%async_computation.11 | async-start | bytes 7077888 | tf_op jit(solution)/shard_map/all_gather | solution.py:231
  97.0 127.6 %copy-start.25 = (f32[768]{0:T(1024)}, f32[768]{0:T(1024)S(1)}, u32[]{:S(2)}) copy-start(f32[768]{0:T(1024)S(1)} %convert_element_type.209) | copy-start | bytes 9220
  97.0 139.6 %copy-start.23 = (f32[768]{0:T(1024)}, f32[768]{0:T(1024)S(1)}, u32[]{:S(2)}) copy-start(f32[768]{0:T(1024)S(1)} %convert_element_type.208) | copy-start | bytes 9220
  97.0 133.3 %copy-start.27 = (f32[768]{0:T(1024)}, f32[768]{0:T(1024)S(1)}, u32[]{:S(2)}) copy-start(f32[768]{0:T(1024)S(1)} %convert_element_type.214) | copy-start | bytes 9220
  122.6 30.3 %copy-start.12 = (bf16[256,768]{1,0:T(8,128)(2,1)S(1)}, bf16[256,768]{1,0:T(8,128)(2,1)}, u32[]{:S(2)}) copy-start(bf16[256,768]{1,0:T(8,128)(2,1)} %param.27) | copy-start | bytes 1179652
  152.7 43.4 %copy-start.15 = (f32[12,256]{1,0:T(8,128)}, f32[12,256]{1,0:T(8,128)S(1)}, u32[]{:S(2)}) copy-start(f32[12,256]{1,0:T(8,128)S(1)} %get-tuple-element.901) | copy-start | bytes 36868
  152.7 43.4 %copy-start.22 = (s32[2048]{0:T(1024)}, s32[2048]{0:T(1024)S(1)}, u32[]{:S(2)}) copy-start(s32[2048]{0:T(1024)S(1)} %get-tuple-element.1721) | copy-start | bytes 24580
  152.8 43.3 %copy-start.8 = (bf16[256,12,64]{0,2,1:T(8,128)(2,1)}, bf16[256,12,64]{0,2,1:T(8,128)(2,1)S(1)}, u32[]{:S(2)}) copy-start(bf16[256,12,64]{0,2,1:T(8,128)(2,1)S(1)} %fusion.70) | copy-start | bytes 1179652
  155.0 81.6 %copy-start.31 = (f32[256]{0:T(256)}, f32[256]{0:T(256)S(1)}, u32[]{:S(2)}) copy-start(f32[256]{0:T(256)S(1)} %broadcast_multiply_fusion.1) | copy-start | bytes 3076
  155.2 81.4 %copy-start.36 = (f32[256]{0:T(256)}, f32[256]{0:T(256)S(1)}, u32[]{:S(2)}) copy-start(f32[256]{0:T(256)S(1)} %fusion.71) | copy-start | bytes 3076
  224.6 6.1 slice-start.2
  224.6 4.7 copy-start.11
  224.6 6.1 slice-start.3
  224.6 6.1 copy-start.49
  229.1 5.2 copy-start
  229.1 2.4 copy-start.48
  229.1 5.2 copy-start.29
  229.3 4.9 copy-start.35
  230.3 4.0 slice-start
  230.6 3.7 copy-start.4
  230.7 3.6 copy-start.38
  231.5 2.9 slice-start.1
  234.3 2.3 copy-start.14
  234.3 2.7 copy-start.6
  237.0 4.8 copy-start.2
  237.0 3.9 copy-start.7
  239.6 251.0 %reduce-scatter.16.cloned.1.call-start = ((), (), s32[]{:S(2)}) async-start(), calls=%async_computation.15 | async-start | bytes 3981312
  271.3 3.7 copy-start.20
  287.0 3.7 copy-start.20
  302.6 3.7 copy-start.20
  327.5 6.8 copy-start.21
  401.2 4.2 copy-start.13
  402.4 2.9 copy-start.17
  414.0 1.2 copy-start.9
  414.0 1.2 copy-start.34
  414.0 3.1 copy-start.24
  414.0 3.1 copy-start.26
  414.0 3.1 copy-start.32
  414.0 3.1 copy-start.37
  414.1 117.1 %reduce-scatter.10.cloned.1.call-start = ((), (), s32[]{:S(2)}) async-start(), calls=%async_computation.12 | async-start | bytes 1327104 | tf_op jit(solution)/shard_map/reduce_scatter | solution.py:314
  416.8 171.5 %reduce-scatter.12.cloned.1.call-start = ((), (), s32[]{:S(2)}) async-start(), calls=%async_computation.13 | async-start | bytes 5308416 | tf_op jit(solution)/shard_map/reduce_scatter | solution.py:326
  422.3 223.3 %reduce-scatter.14.cloned.1.call-start = ((), (), s32[]{:S(2)}) async-start(), calls=%async_computation.14 | async-start | bytes 5308416 | tf_op jit(solution)/shard_map/reduce_scatter | solution.py:332
  428.5 246.0 %copy-start.1 = (f32[256,768]{1,0:T(8,128)S(1)}, f32[256,768]{1,0:T(8,128)}, u32[]{:S(2)}) copy-start(f32[256,768]{1,0:T(8,128)} %copy-done) | copy-start | bytes 2359300
  428.5 246.0 %copy-start.28 = (f32[768]{0:T(1024)S(1)}, f32[768]{0:T(1024)}, u32[]{:S(2)}) copy-start(f32[768]{0:T(1024)} %copy-done.27) | copy-start | bytes 9220
  428.5 246.0 %copy-start.30 = (f32[256]{0:T(256)S(1)}, f32[256]{0:T(256)}, u32[]{:S(2)}) copy-start(f32[256]{0:T(256)} %copy-done.29) | copy-start | bytes 3076
  428.5 247.6 %copy-start.18 = (bf16[256,12,64]{0,2,1:T(8,128)(2,1)S(1)}, bf16[256,12,64]{0,2,1:T(8,128)(2,1)}, u32[]{:S(2)}) copy-start(bf16[256,12,64]{0,2,1:T(8,128)(2,1)} %copy-done.17) | copy-start | bytes 1179652
  428.5 254.2 %reduce-scatter.18.cloned.1.call-start = ((), (), s32[]{:S(2)}) async-start(), calls=%async_computation.16 | async-start | bytes 221184
  432.2 334.4 %all-reduce.19.cloned.1.call-start = ((), (), s32[]{:S(2)}) async-start(), calls=%async_computation.17 | async-start | bytes 3833856 | tf_op jit(solution)/shard_map/psum | solution.py:346
  766.6 6.1 copy-start.16
  (5 other events, 5.0 us)
Sparse Core Ops, SparseCore 0:
  9.9 36.5 all-gather.10
  50.7 32.3 all-gather.12
  85.6 32.1 all-gather.14
  119.5 23.9 all-gather.16
  145.2 38.7 all-gather.18
  185.8 38.7 all-gather.20
  239.7 45.7 all-gather.22
  414.2 76.4 reduce-scatter.15
  494.4 36.6 reduce-scatter.9
  534.5 53.7 reduce-scatter.11
  591.7 53.7 reduce-scatter.13
  649.0 33.6 reduce-scatter.17
  685.9 80.6 all-reduce.18
